TPU v7x, 32 devices: a whole 2x2x4 slice. The times are simulated.
32 devices in a mesh: shot: 8 (over z, y), rcv: 4 (over x, core).
Axes of the slice: x: 2, y: 2, z: 4, core: 2. Of those that a mesh axis runs over, the one named last changes fastest.
Arguments:
- data_matrix: bfloat16 [2, 16, 1024, 1024], P(None, None, 'shot', 'rcv'), may hold values from -12 to 12
- shot_records: bfloat16 [2, 16, 1024, 1024], P(None, None, 'rcv', 'shot'), may hold values from -4 to 4
- live: int32 [1024, 1024], P('rcv', 'shot'), may hold values 0 or 1
Outputs:
- predicted: bfloat16 [2, 16, 1024, 1024], P(None, None, 'rcv', 'shot')
- primaries: bfloat16 [2, 16, 1024, 1024], P(None, None, 'rcv', 'shot')
All inputs are finite; a program needn't handle non-finite values. No bound on the sum of `live` on one device may be relied on, other than what follows from the above.
Results may differ from a plain program's by a relative error of at most 0.013.
Values may be sent and summed in bfloat16 or wider, within the bound.
A program may use at most 128 MiB of HBM per device.

v0:
```python
import jax
import jax.numpy as jnp
from jax import lax
from jax.sharding import PartitionSpec as P


def complex_product(left, right):
    prod = jnp.einsum("afrk,bfks->abfrs", left, right, preferred_element_type=jnp.float32)
    return jnp.stack((prod[0, 0] - prod[1, 1], prod[0, 1] + prod[1, 0]))


def shards(data_matrix, shot_records, live):
    records = shot_records * live.astype(jnp.bfloat16)[None, None]
    own_rows = records.shape[2]
    partial_terms = complex_product(
        lax.all_gather(data_matrix, "shot", axis=2, tiled=True), records
    )
    summed = lax.psum(partial_terms.astype(jnp.bfloat16), "rcv").astype(jnp.float32)
    total = lax.dynamic_slice_in_dim(summed, lax.axis_index("rcv") * own_rows, own_rows, 2)
    rec = records.astype(jnp.float32)
    num_re = jnp.sum(total[0] * rec[0] + total[1] * rec[1], axis=1)
    num_im = jnp.sum(total[0] * rec[1] - total[1] * rec[0], axis=1)
    power = jnp.sum(total[0] * total[0] + total[1] * total[1], axis=1)
    sum_re, sum_im, sum_power = lax.psum((num_re, num_im, power), "rcv")
    points = float(own_rows * lax.axis_size("rcv"))
    power_mean = sum_power / points + 1e-06
    filt_re = (sum_re / points / power_mean)[:, None, :]
    filt_im = (sum_im / points / power_mean)[:, None, :]
    out_re = rec[0] - (filt_re * total[0] - filt_im * total[1])
    out_im = rec[1] - (filt_re * total[1] + filt_im * total[0])
    primaries = jnp.stack((out_re, out_im)).astype(jnp.bfloat16)
    return (total.astype(jnp.bfloat16), primaries)


def solution(mesh):
    in_specs = (P(None, None, "shot", "rcv"), P(None, None, "rcv", "shot"), P("rcv", "shot"))
    out_specs = (P(None, None, "rcv", "shot"), P(None, None, "rcv", "shot"))
    return jax.shard_map(shards, mesh=mesh, in_specs=in_specs, out_specs=out_specs, check_vma=False)
```

profile of v0, /device:TPU:0, one launch (start us, length us, event | category | flops | bytes accessed | tf_op | source)
XLA Modules:
  0.0 466.1 jit_solution(6643771911731964899)
XLA Ops:
  7.2 0.0 all-gather.2.cloned.1.call-start
  7.2 3.1 copy.7
  10.3 0.0 all-gather.2.cloned.1.call-update
  10.4 0.0 copy-start.1
  10.4 0.0 all-reduce.3.cloned.1.call-start
  10.4 1.5 copy-done
  11.9 2.6 copy.6
  14.5 0.0 copy-done.1
  14.5 0.1 copy.5
  14.6 4.0 multiply_convert_fusion
  18.7 222.4 %all-gather.2.cloned.1.call-done = bf16[2,16,1024,256]{3,2,0,1:T(8,128)(2,1)} async-done(((bf16[2,16,128,256]{3,2,0,1:T(8,128)(2,1)}), bf16[2,16,1024,256]{3,2,0,1:T(8,128)(2,1)}) %all-gather.2.cloned.1.call-update) | async-done | bytes 16777232 | tf_op jit(solution)/shard_map/all_gather | solution.py:16
  241.1 17.6 %fusion.2 = f32[2,2,16,1024,128]{3,4,0,1,2:T(8,128)} fusion(bf16[2,16,1024,256]{3,2,0,1:T(8,128)(2,1)} %all-gather.2.cloned.1.call-done, bf16[2,16,256,128,1]{2,3,1,0,4:T(8,128)(2,1)S(1)} %get-tuple-element.15), kind=kOutput, calls=%fused_computation.2 | convolution fusion | flops 4294967296 | bytes 52428800 | tf_op jit(solution)/shard_map/afrk,bfks->abfrs/dot_general | solution.py:8
  258.7 6.6 %fusion.9 = bf16[1,16,1024,128]{2,3,1,0:T(8,128)(2,1)S(1)} fusion(f32[2,2,16,1024,128]{3,4,0,1,2:T(8,128)} %fusion.2), kind=kLoop, calls=%fused_computation.11 | loop fusion | flops 4194304 | bytes 20971520 | tf_op jit(solution)/shard_map/add | solution.py:9
  265.3 8.8 %fusion.8 = bf16[1,16,1024,128]{2,3,1,0:T(8,128)(2,1)} fusion(f32[2,2,16,1024,128]{3,4,0,1,2:T(8,128)} %fusion.2), kind=kLoop, calls=%fused_computation.10 | loop fusion | flops 4194304 | bytes 20971520 | tf_op jit(solution)/shard_map/sub | solution.py:9
  274.0 6.2 %pad_maximum_fusion = bf16[2,16,1024,128]{2,3,1,0:T(8,128)(2,1)} fusion(bf16[1,16,1024,128]{2,3,1,0:T(8,128)(2,1)S(1)} %fusion.9, bf16[1,16,1024,128]{2,3,1,0:T(8,128)(2,1)} %fusion.8), kind=kLoop, calls=%fused_computation.9 | loop fusion | flops 4194304 | bytes 16777216 | tf_op jit(solution)/shard_map/stack | solution.py:9
  280.2 0.0 all-reduce.3.cloned.1.call-update
  280.2 151.2 %all-reduce.3.cloned.1.call-done = bf16[2,16,1024,128]{2,3,1,0:T(8,128)(2,1)} async-done(((bf16[2,16,1024,128]{2,3,1,0:T(8,128)(2,1)}), bf16[2,16,1024,128]{2,3,1,0:T(8,128)(2,1)}) %all-reduce.3.cloned.1.call-update) | async-done | bytes 8388624 | tf_op jit(solution)/shard_map/psum | solution.py:18
  431.4 4.1 dynamic-slice_convert_fusion
  435.5 2.4 copy.11
  437.9 4.6 add_reduce_fusion.1
  442.5 10.3 %all-reduce = (f32[16,128]{1,0:T(8,128)S(1)}, f32[16,128]{1,0:T(8,128)S(1)}, f32[16,128]{1,0:T(8,128)S(1)}) all-reduce(f32[16,128]{1,0:T(8,128)S(1)} %get-tuple-element.5, f32[16,128]{1,0:T(8,128)S(1)} %get-tuple-element.6, f32[16,128]{1,0:T(8,128)S(1)} %get-tuple-element.4), channel_id=1, replica_groups=mesh['shot'=8,'rcv'=4] {'rcv'}, use_global_device_ids=true, to_apply=%region_6.0 | all-reduce | flops 6144 | bytes 49152 | tf_op jit(solution)/shard_map/psum | solution.py:24
  452.8 3.8 subtract_convert_fusion.1
  456.7 0.2 pad_maximum_fusion.1
  456.9 2.4 copy.12
  (3 shorter events, 0.0 us)
Async XLA Ops:
  7.2 233.9 %all-gather.2.cloned.1.call-start = ((), (), s32[]{:S(2)}) async-start(), calls=%async_computation | async-start | bytes 18874368 | tf_op jit(solution)/shard_map/all_gather | solution.py:16
  10.3 1.6 copy-start
  10.4 4.1 copy-start.1
  10.4 421.0 %all-reduce.3.cloned.1.call-start = ((), (), s32[]{:S(2)}) async-start(), calls=%async_computation.1 | async-start | bytes 16777216 | tf_op jit(solution)/shard_map/psum | solution.py:18
Sparse Core Ops, SparseCore 0:
  10.8 230.2 all-gather.1
  280.4 151.0 all-reduce.2
where the time goes:
time: 466 us
  waiting for transfers between devices  374 us (80%)
  other arithmetic  38.4 us (8%)
  matrix products  17.6 us (4%)
  between operations  14.1 us (3%)
  local copies, waits for them, and re-layouts  12.1 us (3%)
  blocking collectives  10.3 us (2%)
    all_gather x1, waiting for transfers between devices, shards(): lax.all_gather(data_matrix, 'shot', axis=2, tiled=True)  222 us
    psum x1, waiting for transfers between devices, shards(): lax.psum(partial_terms.astype(jnp.bfloat16), 'rcv').astype(jnp.float32)  151 us
    dot_general x1, matrix products, complex_product(): jnp.einsum('afrk,bfks->abfrs', left, right, preferred_element_type=jnp.fl...  17.6 us
    unnamed x8, local copies, waits for them, and re-layouts  12 us
    psum x1, blocking collectives, shards(): sum_re, sum_im, sum_power = lax.psum((num_re, num_im, power), 'rcv')  10.3 us
  transfers between devices with their start and end apart: 2, of which 2 were waited for; matrix products, arithmetic and copies ran while one was open for 1% of the time, Pallas kernels for 0%

commit v1 on v0

--- a/solution.py
+++ b/solution.py
@@ -15,7 +15,9 @@
     partial_terms = complex_product(
         lax.all_gather(data_matrix, "shot", axis=2, tiled=True), records
     )
-    summed = lax.psum(partial_terms.astype(jnp.bfloat16), "rcv").astype(jnp.float32)
+    summed = jnp.sum(lax.all_gather(partial_terms.astype(jnp.bfloat16), "rcv"), axis=0).astype(
+        jnp.float32
+    )
     total = lax.dynamic_slice_in_dim(summed, lax.axis_index("rcv") * own_rows, own_rows, 2)
     rec = records.astype(jnp.float32)
     num_re = jnp.sum(total[0] * rec[0] + total[1] * rec[1], axis=1)

time: 466 us -> 533 us (1.14)
  waiting for transfers between devices: 374 us -> 428 us
  other arithmetic: 38.4 us -> 49 us
    all_gather x0 -> x1, waiting for transfers between devices: none -> 200 us  [shards(): lax.all_gather(partial_terms.astype(jnp.bfloat16), 'rcv')]
    psum x1 -> x0, waiting for transfers between devices: 151 us -> none  [shards(): lax.psum(partial_terms.astype(jnp.bfloat16), 'rcv').astype(jnp.float32)]
    reduce_sum x0 -> x1, other arithmetic: none -> 16.4 us  [shards(): jnp.sum(lax.all_gather(partial_terms.astype(jnp.bfloat16), 'rcv'), axis=0)]
    another operation x1 -> x2, other arithmetic: 3.84 us -> 19.6 us
    sub x1 -> x0, other arithmetic: 8.77 us -> none  [complex_product(): return jnp.stack((prod[0, 0] - prod[1, 1], prod[0, 1] + prod[1, 0]))]
    add x1 -> x0, other arithmetic: 6.6 us -> none  [complex_product(): return jnp.stack((prod[0, 0] - prod[1, 1], prod[0, 1] + prod[1, 0]))]
    unnamed x8 -> x10, local copies, waits for them, and re-layouts: 12 us -> 14.3 us
where the time goes in v1:
time: 533 us
  waiting for transfers between devices  428 us (80%)
  other arithmetic  49 us (9%)
  matrix products  17.6 us (3%)
  local copies, waits for them, and re-layouts  14.4 us (3%)
  between operations  14.1 us (3%)
  blocking collectives  10.3 us (2%)
    all_gather x1, waiting for transfers between devices, shards(): lax.all_gather(data_matrix, 'shot', axis=2, tiled=True)  228 us
    all_gather x1, waiting for transfers between devices, shards(): lax.all_gather(partial_terms.astype(jnp.bfloat16), 'rcv')  200 us
    another operation x2, other arithmetic  19.6 us
    dot_general x1, matrix products, complex_product(): jnp.einsum('afrk,bfks->abfrs', left, right, preferred_element_type=jnp.fl...  17.6 us
    reduce_sum x1, other arithmetic, shards(): jnp.sum(lax.all_gather(partial_terms.astype(jnp.bfloat16), 'rcv'), axis=0)  16.4 us
    unnamed x10, local copies, waits for them, and re-layouts  14.3 us
  transfers between devices with their start and end apart: 2, of which 2 were waited for; matrix products, arithmetic and copies ran while one was open for 1% of the time, Pallas kernels for 0%

profile of v1, /device:TPU:0, one launch (start us, length us, event | category | flops | bytes accessed | tf_op | source)
XLA Modules:
  0.0 533.0 jit_solution(10698261718985932182)
XLA Ops:
  7.2 0.0 all-gather.3.cloned.1.call-start
  7.2 3.1 copy.9
  10.3 0.0 all-gather.3.cloned.1.call-update
  10.4 0.0 copy-start.2
  10.4 0.0 all-gather.5.cloned.1.call-start
  10.4 2.9 copy.8
  13.3 0.0 copy-done.2
  13.3 0.1 copy.7
  13.4 227.6 %all-gather.3.cloned.1.call-done = bf16[2,16,1024,256]{3,2,0,1:T(8,128)(2,1)} async-done(((bf16[2,16,128,256]{3,2,0,1:T(8,128)(2,1)}), bf16[2,16,1024,256]{3,2,0,1:T(8,128)(2,1)}) %all-gather.3.cloned.1.call-update) | async-done | bytes 16777232 | tf_op jit(solution)/shard_map/all_gather | solution.py:16
  241.1 17.6 %fusion.2 = f32[2,2,16,1024,128]{3,4,0,1,2:T(8,128)} fusion(bf16[2,16,1024,256]{3,2,0,1:T(8,128)(2,1)} %all-gather.3.cloned.1.call-done, bf16[2,16,256,128]{2,3,0,1:T(8,128)(2,1)S(1)} %copy.8, bf16[256,128]{0,1:T(8,128)(2,1)S(1)} %copy.7), kind=kOutput, calls=%fused_computation.2 | convolution fusion | flops 4299161600 | bytes 52494336 | tf_op jit(solution)/shard_map/afrk,bfks->abfrs/dot_general | solution.py:8
  258.7 15.7 %fusion.6 = (bf16[1,1,16,1024,128]{3,4,0,1,2:T(8,128)(2,1)}, bf16[1,1,16,1024,128]{3,4,0,1,2:T(8,128)(2,1)}) fusion(f32[2,2,16,1024,128]{3,4,0,1,2:T(8,128)} %fusion.2), kind=kLoop, calls=%fused_computation.6 | loop fusion | flops 8388608 | bytes 41943040 | tf_op jit(solution)/shard_map/convert.3
  274.4 7.4 %pad_maximum_fusion = bf16[1,2,16,1024,128]{3,4,0,1,2:T(8,128)(2,1)} fusion(bf16[1,1,16,1024,128]{3,4,0,1,2:T(8,128)(2,1)} %get-tuple-element.11, bf16[1,1,16,1024,128]{3,4,0,1,2:T(8,128)(2,1)} %get-tuple-element.10), kind=kLoop, calls=%fused_computation.7 | loop fusion | flops 4194304 | bytes 16777216 | tf_op jit(solution)/shard_map/stack | solution.py:9
  281.8 0.0 all-gather.5.cloned.1.call-update
  281.9 199.9 %all-gather.5.cloned.1.call-done = bf16[4,2,16,1024,128]{3,4,0,1,2:T(8,128)(2,1)} async-done(((bf16[1,2,16,1024,128]{3,4,0,1,2:T(8,128)(2,1)}), bf16[4,2,16,1024,128]{3,4,0,1,2:T(8,128)(2,1)}) %all-gather.5.cloned.1.call-update) | async-done | bytes 33554448 | tf_op jit(solution)/shard_map/all_gather | solution.py:18
  481.7 16.4 %reduce_sum.39 = bf16[2,16,1024,128]{2,3,0,1:T(8,128)(2,1)} reduce(bf16[4,2,16,1024,128]{3,4,0,1,2:T(8,128)(2,1)} %all-gather.5.cloned.1.call-done, bf16[]{:T(256)} %constant.5.clone.1), dimensions={0}, to_apply=%region_0.0 | reduce | flops 12582912 | bytes 41943040 | tf_op jit(solution)/shard_map/reduce_sum | solution.py:18
  498.1 4.2 dynamic-slice_convert_fusion
  502.3 1.2 add_reduce_fusion.1
  503.5 0.8 copy-done
  504.2 1.2 copy-done.1
  505.5 10.3 %all-reduce = (f32[16,128]{1,0:T(8,128)S(1)}, f32[16,128]{1,0:T(8,128)S(1)}, f32[16,128]{1,0:T(8,128)S(1)}) all-reduce(f32[16,128]{1,0:T(8,128)S(1)} %get-tuple-element.5, f32[16,128]{1,0:T(8,128)S(1)} %get-tuple-element.6, f32[16,128]{1,0:T(8,128)S(1)} %get-tuple-element.4), channel_id=1, replica_groups=mesh['shot'=8,'rcv'=4] {'rcv'}, use_global_device_ids=true, to_apply=%region_6.0 | all-reduce | flops 6144 | bytes 49152 | tf_op jit(solution)/shard_map/psum | solution.py:26
  515.8 3.9 subtract_convert_fusion.1
  519.7 0.2 pad_maximum_fusion.1
  519.9 2.4 copy.11
  522.3 3.9 copy.10
  (4 shorter events, 0.0 us)
Async XLA Ops:
  7.2 233.9 %all-gather.3.cloned.1.call-start = ((), (), s32[]{:S(2)}) async-start(), calls=%async_computation | async-start | bytes 18874368 | tf_op jit(solution)/shard_map/all_gather | solution.py:16
  10.4 2.9 copy-start.2
  10.4 471.3 %all-gather.5.cloned.1.call-start = ((), (), s32[]{:S(2)}) async-start(), calls=%async_computation.1 | async-start | bytes 41943040 | tf_op jit(solution)/shard_map/all_gather | solution.py:18
  502.3 2.0 copy-start
  502.3 3.2 copy-start.1
Sparse Core Ops, SparseCore 0:
  10.8 230.2 all-gather.2
  282.0 199.7 all-gather.4

commit v2 on v0

--- a/solution.py
+++ b/solution.py
@@ -2,6 +2,27 @@
 import jax.numpy as jnp
 from jax import lax
 from jax.sharding import PartitionSpec as P
+
+
+def ring_gather(x, axis, dim):
+    size, here, span = (lax.axis_size(axis), lax.axis_index(axis), x.shape[dim])
+    right = [(i, (i + 1) % size) for i in range(size)]
+    left = [(i, (i - 1) % size) for i in range(size)]
+    whole = jnp.zeros((*x.shape[:dim], size * span, *x.shape[dim + 1 :]), x.dtype)
+    whole = lax.dynamic_update_slice_in_dim(whole, x, here * span, axis=dim)
+    from_left = from_right = x
+    middle = size // 2
+    for step in range(1, middle + 1):
+        from_left = lax.ppermute(from_left, axis, right)
+        whole = lax.dynamic_update_slice_in_dim(
+            whole, from_left, (here - step) % size * span, axis=dim
+        )
+        if step < size - middle:
+            from_right = lax.ppermute(from_right, axis, left)
+            whole = lax.dynamic_update_slice_in_dim(
+                whole, from_right, (here + step) % size * span, axis=dim
+            )
+    return whole
 
 
 def complex_product(left, right):
@@ -12,9 +33,7 @@
 def shards(data_matrix, shot_records, live):
     records = shot_records * live.astype(jnp.bfloat16)[None, None]
     own_rows = records.shape[2]
-    partial_terms = complex_product(
-        lax.all_gather(data_matrix, "shot", axis=2, tiled=True), records
-    )
+    partial_terms = complex_product(ring_gather(data_matrix, "shot", 2), records)
     summed = lax.psum(partial_terms.astype(jnp.bfloat16), "rcv").astype(jnp.float32)
     total = lax.dynamic_slice_in_dim(summed, lax.axis_index("rcv") * own_rows, own_rows, 2)
     rec = records.astype(jnp.float32)

time: 466 us -> 562 us (1.21)
  waiting for transfers between devices: 374 us -> 423 us
  local copies, waits for them, and re-layouts: 12.1 us -> 37.4 us
  starting transfers between devices: 0.08 us -> 19.7 us
    ppermute x0 -> x7, waiting for transfers between devices: none -> 271 us  [the longest x4 271 us: ring_gather(): from_left = lax.ppermute(from_left, axis, right)]
    all_gather x1 -> x0, waiting for transfers between devices: 222 us -> none  [shards(): lax.all_gather(data_matrix, 'shot', axis=2, tiled=True)]
    dynamic_update_slice x0 -> x8, local copies, waits for them, and re-layouts: none -> 21.5 us  [the longest x4 12.5 us: ring_gather(): lax.dynamic_update_slice_in_dim(whole, from_left, (here - step) % size *...]
    ppermute x0 -> x7, starting transfers between devices: none -> 19.7 us  [the longest x4 10.5 us: ring_gather(): from_left = lax.ppermute(from_left, axis, right)]
    broadcast_in_dim x0 -> x1, local copies, waits for them, and re-layouts: none -> 5.84 us  [ring_gather(): jnp.zeros((*x.shape[:dim], size * span, *x.shape[dim + 1:]), x.dtype)]
    unnamed x8 -> x11, local copies, waits for them, and re-layouts: 12 us -> 10 us
  transfers between devices with their start and end apart: 2 -> 8, of which waited for: 2 -> 5; matrix products, arithmetic and copies ran while one was open for 1% -> 6% of each run, Pallas kernels for 0% -> 0%
where the time goes in v2:
time: 562 us; the launch traced here: 561 us
  waiting for transfers between devices  423 us (75%)
  other arithmetic  39.3 us (7%)
  local copies, waits for them, and re-layouts  37.4 us (7%)
  starting transfers between devices  19.7 us (4%)
  matrix products  17.6 us (3%)
  between operations  14.1 us (3%)
  blocking collectives  10.3 us (2%)
    ppermute x4, waiting for transfers between devices, ring_gather(): from_left = lax.ppermute(from_left, axis, right)  271 us
    psum x1, waiting for transfers between devices, shards(): lax.psum(partial_terms.astype(jnp.bfloat16), 'rcv').astype(jnp.float32)  151 us
    dot_general x1, matrix products, complex_product(): jnp.einsum('afrk,bfks->abfrs', left, right, preferred_element_type=jnp.fl...  17.6 us
    dynamic_update_slice x4, local copies, waits for them, and re-layouts, ring_gather(): lax.dynamic_update_slice_in_dim(whole, from_left, (here - step) % size *...  12.5 us
  transfers between devices with their start and end apart: 8, of which 5 were waited for; matrix products, arithmetic and copies ran while one was open for 6% of the time, Pallas kernels for 0%

profile of v2, /device:TPU:0, one launch (start us, length us, event | category | flops | bytes accessed | tf_op | source)
XLA Modules:
  0.0 561.3 jit_solution(9740877775313810079)
XLA Ops:
  10.2 3.1 collective-permute-start.1
  13.3 87.0 %collective-permute-done = bf16[2,16,128,256]{3,2,1,0:T(8,128)(2,1)S(1)} collective-permute-done((bf16[2,16,128,256]{3,2,1,0:T(8,128)(2,1)}, bf16[2,16,128,256]{3,2,1,0:T(8,128)(2,1)S(1)}, u32[]{:S(2)}, u32[]{:S(2)}) %collective-permute-start) | collective-permute-done | bytes 2097184 | tf_op jit(solution)/shard_map/ppermute | solution.py:16
  104.1 3.1 collective-permute-start.3
  107.2 85.9 %collective-permute-done.2 = bf16[2,16,128,256]{3,2,1,0:T(8,128)(2,1)} collective-permute-done((bf16[2,16,128,256]{3,2,1,0:T(8,128)(2,1)S(1)}, bf16[2,16,128,256]{3,2,1,0:T(8,128)(2,1)}, u32[]{:S(2)}, u32[]{:S(2)}) %collective-permute-start.2) | collective-permute-done | bytes 2097184 | tf_op jit(solution)/shard_map/ppermute | solution.py:16
  196.6 3.9 copy.6
  203.6 4.0 multiply_convert_fusion
  207.7 76.9 %collective-permute-done.4 = bf16[2,16,128,256]{3,2,1,0:T(8,128)(2,1)} collective-permute-done((bf16[2,16,128,256]{3,2,1,0:T(8,128)(2,1)}, bf16[2,16,128,256]{3,2,1,0:T(8,128)(2,1)}, u32[]{:S(2)}, u32[]{:S(2)}) %collective-permute-start.4) | collective-permute-done | bytes 2097184 | tf_op jit(solution)/shard_map/ppermute | solution.py:16
  287.1 5.8 %broadcast_in_dim.2 = bf16[2,16,1024,256]{3,2,0,1:T(8,128)(2,1)} broadcast(bf16[]{:T(256)} %constant.59.clone.1), dimensions={} | broadcast | bytes 16777218 | tf_op jit(solution)/shard_map/broadcast_in_dim | solution.py:11
  294.3 3.2 copy_dynamic-update-slice_fusion.6
  298.9 3.1 copy_dynamic-update-slice_fusion.4
  302.0 3.1 copy_dynamic-update-slice_fusion.3
  305.1 3.1 copy_dynamic-update-slice_fusion.2
  308.2 3.1 copy_dynamic-update-slice_fusion.1
  311.3 21.6 %collective-permute-done.6 = bf16[2,16,128,256]{3,2,1,0:T(8,128)(2,1)} collective-permute-done((bf16[2,16,128,256]{3,2,1,0:T(8,128)(2,1)}, bf16[2,16,128,256]{3,2,1,0:T(8,128)(2,1)}, u32[]{:S(2)}, u32[]{:S(2)}) %collective-permute-start.6) | collective-permute-done | bytes 2097184 | tf_op jit(solution)/shard_map/ppermute | solution.py:16
  332.9 3.1 copy_dynamic-update-slice_fusion
  336.0 17.6 %fusion.2 = f32[2,2,16,1024,128]{3,4,0,1,2:T(8,128)} fusion(bf16[2,16,1024,256]{3,2,0,1:T(8,128)(2,1)} %copy_dynamic-update-slice_fusion, bf16[2,16,256,128,1]{2,3,1,0,4:T(8,128)(2,1)S(1)} %get-tuple-element.15), kind=kOutput, calls=%fused_computation.2 | convolution fusion | flops 4294967296 | bytes 52428800 | tf_op jit(solution)/shard_map/afrk,bfks->abfrs/dot_general | solution.py:29
  353.6 6.6 %fusion.9 = bf16[1,16,1024,128]{2,3,1,0:T(8,128)(2,1)S(1)} fusion(f32[2,2,16,1024,128]{3,4,0,1,2:T(8,128)} %fusion.2), kind=kLoop, calls=%fused_computation.11 | loop fusion | flops 4194304 | bytes 20971520 | tf_op jit(solution)/shard_map/add | solution.py:30
  360.2 8.8 %fusion.8 = bf16[1,16,1024,128]{2,3,1,0:T(8,128)(2,1)} fusion(f32[2,2,16,1024,128]{3,4,0,1,2:T(8,128)} %fusion.2), kind=kLoop, calls=%fused_computation.10 | loop fusion | flops 4194304 | bytes 20971520 | tf_op jit(solution)/shard_map/sub | solution.py:30
  368.9 6.2 %pad_maximum_fusion = bf16[2,16,1024,128]{2,3,1,0:T(8,128)(2,1)} fusion(bf16[1,16,1024,128]{2,3,1,0:T(8,128)(2,1)S(1)} %fusion.9, bf16[1,16,1024,128]{2,3,1,0:T(8,128)(2,1)} %fusion.8), kind=kLoop, calls=%fused_computation.9 | loop fusion | flops 4194304 | bytes 16777216 | tf_op jit(solution)/shard_map/stack | solution.py:30
  375.1 151.5 %all-reduce.3.cloned.1.call-done = bf16[2,16,1024,128]{2,3,1,0:T(8,128)(2,1)} async-done(((bf16[2,16,1024,128]{2,3,1,0:T(8,128)(2,1)}), bf16[2,16,1024,128]{2,3,1,0:T(8,128)(2,1)}) %all-reduce.3.cloned.1.call-update) | async-done | bytes 8388624 | tf_op jit(solution)/shard_map/psum | solution.py:37
  526.6 4.1 dynamic-slice_convert_fusion
  533.1 4.6 add_reduce_fusion.1
  537.7 10.3 %all-reduce = (f32[16,128]{1,0:T(8,128)S(1)}, f32[16,128]{1,0:T(8,128)S(1)}, f32[16,128]{1,0:T(8,128)S(1)}) all-reduce(f32[16,128]{1,0:T(8,128)S(1)} %get-tuple-element.5, f32[16,128]{1,0:T(8,128)S(1)} %get-tuple-element.6, f32[16,128]{1,0:T(8,128)S(1)} %get-tuple-element.4), channel_id=1, replica_groups=mesh['shot'=8,'rcv'=4] {'rcv'}, use_global_device_ids=true, to_apply=%region_6.7 | all-reduce | flops 6144 | bytes 49152 | tf_op jit(solution)/shard_map/psum | solution.py:43
  548.0 3.8 subtract_convert_fusion.1
  (26 shorter events, 23.7 us)
Async XLA Ops:
  7.2 519.5 %all-reduce.3.cloned.1.call-start = ((), (), s32[]{:S(2)}) async-start(), calls=%async_computation | async-start | bytes 16777216 | tf_op jit(solution)/shard_map/psum | solution.py:37
  7.2 93.2 %collective-permute-start = (bf16[2,16,128,256]{3,2,1,0:T(8,128)(2,1)}, bf16[2,16,128,256]{3,2,1,0:T(8,128)(2,1)S(1)}, u32[]{:S(2)}, u32[]{:S(2)}) collective-permute-start(bf16[2,16,128,256]{3,2,1,0:T(8,128)(2,1)} %param.3), channel_id=1, source_target_pairs={{0,4},{4,8},{8,12},{12,16},{16,20},{20,24},{24,28},{28,0},{1,5},{5... | collective-permute-start | bytes 6291464 | tf_op jit(solution)/shard_map/ppermute | solution.py:16
  10.2 93.8 %collective-permute-start.1 = (bf16[2,16,128,256]{3,2,1,0:T(8,128)(2,1)}, bf16[2,16,128,256]{3,2,1,0:T(8,128)(2,1)S(1)}, u32[]{:S(2)}, u32[]{:S(2)}) collective-permute-start(bf16[2,16,128,256]{3,2,1,0:T(8,128)(2,1)} %param.3), channel_id=1, source_target_pairs={{0,28},{4,0},{8,4},{12,8},{16,12},{20,16},{24,20},{28,24},{1,29},{... | collective-permute-start | bytes 6291464 | tf_op jit(solution)/shard_map/ppermute | solution.py:21
  100.4 1.3 copy-start.1
  101.7 91.3 %collective-permute-start.2 = (bf16[2,16,128,256]{3,2,1,0:T(8,128)(2,1)S(1)}, bf16[2,16,128,256]{3,2,1,0:T(8,128)(2,1)}, u32[]{:S(2)}, u32[]{:S(2)}) collective-permute-start(bf16[2,16,128,256]{3,2,1,0:T(8,128)(2,1)S(1)} %collective-permute-done), channel_id=1, source_target_pairs={{0,4},{4,8},{8,12},{12,16},{16,20},{20,24},{24,28},{28,0},{1,5},{5... | collective-permute-start | bytes 6291464 | tf_op jit(solution)/shard_map/ppermute | solution.py:16
  104.1 96.5 %copy-start.2 = (bf16[2,16,128,256]{3,2,1,0:T(8,128)(2,1)}, bf16[2,16,128,256]{3,2,1,0:T(8,128)(2,1)S(1)}, u32[]{:S(2)}) copy-start(bf16[2,16,128,256]{3,2,1,0:T(8,128)(2,1)S(1)} %collective-permute-done.1) | copy-start | bytes 6291460
  104.1 96.5 %collective-permute-start.3 = (bf16[2,16,128,256]{3,2,1,0:T(8,128)(2,1)S(1)}, bf16[2,16,128,256]{3,2,1,0:T(8,128)(2,1)}, u32[]{:S(2)}, u32[]{:S(2)}) collective-permute-start(bf16[2,16,128,256]{3,2,1,0:T(8,128)(2,1)S(1)} %collective-permute-done.1), channel_id=1, source_target_pairs={{0,28},{4,0},{8,4},{12,8},{16,12},{20,16},{24,20},{28,24},{1,29},{... | collective-permute-start | bytes 6291464 | tf_op jit(solution)/shard_map/ppermute | solution.py:21
  193.0 91.6 %collective-permute-start.4 = (bf16[2,16,128,256]{3,2,1,0:T(8,128)(2,1)}, bf16[2,16,128,256]{3,2,1,0:T(8,128)(2,1)}, u32[]{:S(2)}, u32[]{:S(2)}) collective-permute-start(bf16[2,16,128,256]{3,2,1,0:T(8,128)(2,1)} %collective-permute-done.2), channel_id=1, source_target_pairs={{0,4},{4,8},{8,12},{12,16},{16,20},{20,24},{24,28},{28,0},{1,5},{5... | collective-permute-start | bytes 6291464 | tf_op jit(solution)/shard_map/ppermute | solution.py:16
  200.6 107.6 %collective-permute-start.5 = (bf16[2,16,128,256]{3,2,1,0:T(8,128)(2,1)}, bf16[2,16,128,256]{3,2,1,0:T(8,128)(2,1)}, u32[]{:S(2)}, u32[]{:S(2)}) collective-permute-start(bf16[2,16,128,256]{3,2,1,0:T(8,128)(2,1)} %collective-permute-done.3), channel_id=1, source_target_pairs={{0,28},{4,0},{8,4},{12,8},{16,12},{20,16},{24,20},{28,24},{1,29},{... | collective-permute-start | bytes 6291464 | tf_op jit(solution)/shard_map/ppermute | solution.py:21
  207.7 85.2 %copy-start = (bf16[2,16,128,256]{3,2,1,0:T(8,128)(2,1)S(1)}, bf16[2,16,128,256]{3,2,1,0:T(8,128)(2,1)}, u32[]{:S(2)}) copy-start(bf16[2,16,128,256]{3,2,1,0:T(8,128)(2,1)} %param.3) | copy-start | bytes 6291460
  284.6 48.3 %collective-permute-start.6 = (bf16[2,16,128,256]{3,2,1,0:T(8,128)(2,1)}, bf16[2,16,128,256]{3,2,1,0:T(8,128)(2,1)}, u32[]{:S(2)}, u32[]{:S(2)}) collective-permute-start(bf16[2,16,128,256]{3,2,1,0:T(8,128)(2,1)} %collective-permute-done.4), channel_id=1, source_target_pairs={{0,4},{4,8},{8,12},{12,16},{16,20},{20,24},{24,28},{28,0},{1,5},{5... | collective-permute-start | bytes 6291464 | tf_op jit(solution)/shard_map/ppermute | solution.py:16
  294.3 3.2 copy-start.3
Sparse Core Ops, SparseCore 0:
  375.3 151.3 all-reduce.2
